TPU v7x, 32 devices: a whole 2x2x4 slice. The times are simulated.
32 devices in a mesh: ctx: 4 (over z), ep: 8 (over y, x, core).
Axes of the slice: x: 2, y: 2, z: 4, core: 2. Of those that a mesh axis runs over, the one named last changes fastest.
Arguments:
- out_grad: bfloat16 [64, 3584], P(('ctx', 'ep')), may hold values from -6 to 6
- expert_ids: int32 [64, 8], P(('ctx', 'ep')), may hold values from 0 to 31, all different within a row; in each aligned block of 16 rows (0 to 15, 16 to 31, ...) at most 7 rows name the same one
- gate_values: float32 [64, 8], P(('ctx', 'ep')), may hold values from 0.1 to 2.5
- hidden: bfloat16 [4, 32, 7, 1536], P(None, 'ep', None, 'ctx'), may hold values from -0.29882812 to 0.29882812
- w_down: bfloat16 [32, 1536, 3584], P('ep', 'ctx'), may hold values from -0.15625 to 0.15625
Outputs:
- hidden_grad: bfloat16 [4, 32, 7, 1536], P(None, 'ep', None, 'ctx')
- weight_grad: bfloat16 [32, 1536, 3584], P('ep', 'ctx')
- gate_grad: float32 [64, 8], P(('ctx', 'ep'))
Inputs may be any that keep to these rules, and one draw needn't show every extreme that they name: `expert_ids`: each token names 8 different experts. In each aligned block of 16 tokens no expert is named by more than 7 tokens.
All inputs are finite; a program needn't handle non-finite values.
Results may differ from a plain program's by a relative error of at most 0.012.
Values may be sent and summed in bfloat16 or wider, within the bound.
A program may use at most 64 MiB of HBM per device.

v0:
```python
import jax
import jax.numpy as jnp
from jax import lax
from jax.sharding import PartitionSpec as P


def route_places(group_ids, experts_all, capacity):
    flat_ids = group_ids.reshape(-1)
    onehot = (flat_ids[:, None] == jnp.arange(experts_all, dtype=jnp.int32)[None, :]).astype(
        jnp.int32
    )
    before = jnp.cumsum(onehot, axis=0) - onehot
    slot_index = jnp.sum(before * onehot, axis=1)
    return (flat_ids * capacity + slot_index).astype(jnp.int32)


def per_device(out_grad, expert_ids, gate_values, hidden, w_down):
    tok_dev, top_count = expert_ids.shape
    groups, exp_dev, capacity, width_part = hidden.shape
    model_width = out_grad.shape[1]
    ep_count = lax.axis_size("ep")
    ep_rank = lax.axis_index("ep")
    slots_dev = exp_dev * capacity
    experts_all = exp_dev * ep_count
    own_first = ep_rank * slots_dev
    slot_range = jnp.arange(slots_dev, dtype=jnp.int32)
    group_rows, group_ids, group_gates = (
        lax.all_gather(out_grad, "ep", axis=0, tiled=True),
        lax.all_gather(expert_ids, "ep", axis=0, tiled=True),
        lax.all_gather(gate_values.astype(jnp.bfloat16), "ep", axis=0, tiled=True).astype(
            gate_values.dtype
        ),
    )
    places = route_places(group_ids, experts_all, capacity)
    own_places = lax.dynamic_slice_in_dim(
        places, ep_rank * tok_dev * top_count, tok_dev * top_count
    )
    local_slot = places - own_first
    pick_mask = (local_slot[None, :] == slot_range[:, None]).astype(jnp.float32)
    slot_gates = jnp.sum(pick_mask * group_gates.reshape(1, -1), axis=1)
    by_token = pick_mask.reshape(slots_dev, -1, top_count).sum(axis=2).astype(jnp.bfloat16)
    slot_rows = jnp.dot(by_token, group_rows, preferred_element_type=jnp.float32).astype(
        jnp.bfloat16
    )
    stacked_rows = slot_rows.reshape(1, slots_dev, model_width)
    stacked_gates = slot_gates.reshape(1, slots_dev)
    whole_rows, whole_gates = (
        lax.all_gather(stacked_rows, "ctx", axis=0, tiled=True),
        lax.all_gather(stacked_gates.astype(jnp.bfloat16), "ctx", axis=0, tiled=True).astype(
            stacked_gates.dtype
        ),
    )
    row_count = whole_rows.shape[0]
    piece_view = whole_rows.reshape(row_count, exp_dev, capacity, model_width)
    gate_view = whole_gates.reshape(row_count, exp_dev, capacity)
    grad_in = jnp.einsum("necd,efd->necf", piece_view, w_down, preferred_element_type=jnp.float32)
    hid_piece = (gate_view[..., None] * grad_in).astype(jnp.bfloat16)
    gate_piece = jnp.sum(hidden.astype(jnp.float32) * grad_in, axis=3)
    scaled = (gate_view[..., None] * piece_view.astype(jnp.float32)).astype(jnp.bfloat16)
    grad_acc = jnp.einsum("necf,necd->efd", hidden, scaled, preferred_element_type=jnp.float32)
    hid_grad = hid_piece
    partial_value = gate_piece
    grad_acc, hid_grad, partial_value = (grad_acc, hid_grad, partial_value)
    whole_terms = lax.psum(partial_value, "ctx")
    own_terms = lax.dynamic_slice_in_dim(whole_terms, lax.axis_index("ctx"), 1, 0)
    score_table = lax.all_gather(own_terms.reshape(slots_dev), "ep", axis=0, tiled=True)
    lookup = (
        own_places[:, None] == jnp.arange(score_table.shape[0], dtype=jnp.int32)[None, :]
    ).astype(jnp.float32)
    gate_grad = jnp.sum(lookup * score_table[None, :], axis=1).reshape(tok_dev, top_count)
    return (hid_grad, grad_acc.astype(jnp.bfloat16), gate_grad)


def solution(mesh):
    placed = (
        P(("ctx", "ep"), None),
        P(("ctx", "ep"), None),
        P(("ctx", "ep"), None),
        P(None, "ep", None, "ctx"),
        P("ep", "ctx", None),
    )
    return jax.shard_map(
        per_device,
        mesh=mesh,
        in_specs=placed,
        out_specs=(P(None, "ep", None, "ctx"), P("ep", "ctx", None), P(("ctx", "ep"), None)),
        check_vma=False,
    )
```

profile of v0, /device:TPU:0, one launch (start us, length us, event | category | flops | bytes accessed | tf_op | source)
XLA Modules:
  0.0 119.2 jit_solution(10232744558941915128)
XLA Ops:
  0.6 0.0 copy-start
  0.7 1.3 %dynamic-slice.1 = u32[1]{0:T(128)} dynamic-slice(u32[32]{0:T(128)} %constant.42, u32[]{:T(128)S(6)} %add.22), dynamic_slice_sizes={1} | dynamic-slice | bytes 12
  2.6 1.2 %dynamic-slice = u32[1]{0:T(128)} dynamic-slice(u32[32]{0:T(128)} %constant.37, u32[]{:T(128)S(6)} %add.22), dynamic_slice_sizes={1} | dynamic-slice | bytes 12
  4.5 0.7 convert_bitcast_fusion
  5.2 10.3 %all-gather.3 = bf16[8,2,8]{2,1,0:T(2,128)(2,1)S(1)} all-gather(bf16[1,2,8]{2,1,0:T(2,128)(2,1)S(1)} %convert_bitcast_fusion), channel_id=1, replica_groups=mesh['ctx'=4,'ep'=8] {'ep'}, dimensions={0}, use_global_device_ids=true | all-gather | bytes 288 | tf_op jit(solution)/shard_map/all_gather | solution.py:30
  15.4 0.1 reshape.61
  15.5 8.9 %all-gather.2 = s32[8,2,8]{2,1,0:T(2,128)S(1)} all-gather(s32[1,2,8]{2,1,0:T(2,128)} %bitcast.35), channel_id=1, replica_groups=mesh['ctx'=4,'ep'=8] {'ep'}, dimensions={0}, use_global_device_ids=true | all-gather | bytes 576 | tf_op jit(solution)/shard_map/all_gather | solution.py:29
  24.4 0.1 reshape.56
  24.5 0.1 fusion.9
  24.6 0.2 reduce_window_sum.11
  24.8 0.2 select_reduce_fusion
  25.0 0.1 select_reduce_fusion.2
  25.1 0.2 dynamic-update-slice
  25.4 11.9 %all-reduce = bf16[112]{0:T(256)(128)(2,1)S(1)} all-reduce(bf16[112]{0:T(256)(128)(2,1)S(1)} %dynamic-update-slice), channel_id=2, replica_groups=mesh['ctx'=4,'ep'=8] {'ctx'}, use_global_device_ids=true, to_apply=%add | all-reduce | flops 112 | bytes 448
  37.3 0.1 dynamic_slice.6
  37.4 0.1 reshape.62
  37.5 0.1 reduce_sum.49
  37.6 0.1 convert_reduce_fusion
  37.7 0.1 copy.33
  37.8 8.4 %all-gather.4 = bf16[8,2,3584]{2,1,0:T(2,128)(2,1)S(1)} all-gather(bf16[1,2,3584]{2,1,0:T(2,128)(2,1)} %bitcast.34), channel_id=1, replica_groups=mesh['ctx'=4,'ep'=8] {'ep'}, dimensions={0}, use_global_device_ids=true | all-gather | bytes 129024 | tf_op jit(solution)/shard_map/all_gather | solution.py:28
  46.3 0.2 fusion.3
  46.5 19.8 %all-gather.5 = bf16[4,28,3584]{2,1,0:T(8,128)(2,1)S(1)} all-gather(bf16[1,28,3584]{2,1,0:T(8,128)(2,1)S(1)} %fusion.3), channel_id=3, replica_groups=mesh['ctx'=4,'ep'=8] {'ctx'}, dimensions={0}, use_global_device_ids=true | all-gather | bytes 1003520 | tf_op jit(solution)/shard_map/all_gather | solution.py:48
  66.3 0.6 copy.34
  67.0 7.6 %multiply_reduce_fusion = (f32[4,4,7]{0,2,1:T(8,128)S(1)}, bf16[4,4,7,384]{3,0,2,1:T(4,128)(2,1)S(1)}) fusion(bf16[4,4,7,384]{3,1,2,0:T(4,128)(2,1)} %param.8, f32[4,4,7]{0,2,1:T(8,128)S(1)} %copy.33, bf16[4,4,7,3584]{3,0,2,1:T(4,128)(2,1)S(1)} %bitcast.31, bf16[4,384,3584]{2,1,0:T(8,128)(2,1)} %param.9), kind=kOutput, calls=%fused_computation.9 | convolution fusion | flops 308496256 | bytes 11985792 | tf_op jit(solution)/shard_map/necd,efd->necf/dot_general | solution.py:56
  74.6 0.1 copy.43
  74.7 10.0 %psum.7 = f32[4,4,7]{2,0,1:T(4,128)S(1)} all-reduce(f32[4,4,7]{2,0,1:T(4,128)S(1)} %copy.43), channel_id=1, replica_groups=mesh['ctx'=4,'ep'=8] {'ctx'}, use_global_device_ids=true, to_apply=%region_5.6 | all-reduce | flops 112 | bytes 896 | tf_op jit(solution)/shard_map/psum | solution.py:64
  84.7 0.1 reshape.71
  84.7 0.2 dynamic-update-slice.1
  84.9 11.8 %all-reduce.1 = f32[224]{0:T(256)S(1)} all-reduce(f32[224]{0:T(256)S(1)} %dynamic-update-slice.1), channel_id=1, replica_groups=mesh['ctx'=4,'ep'=8] {'ep'}, use_global_device_ids=true, to_apply=%add.1 | all-reduce | flops 224 | bytes 1792
  96.7 0.2 select_reduce_fusion.1
  96.9 0.6 reshape.60
  97.5 0.7 copy.39
  98.2 0.0 copy-done
  98.2 6.3 %fusion = bf16[4,384,3584]{1,2,0:T(8,128)(2,1)} fusion(bf16[4,4,7,3584]{3,0,2,1:T(4,128)(2,1)S(1)} %bitcast.32, f32[4,4,7]{0,2,1:T(8,128)S(1)} %copy.33, bf16[4,4,7,384]{3,1,2,0:T(4,128)(2,1)S(1)} %copy-done), kind=kOutput, calls=%fused_computation.1 | convolution fusion | flops 314990592 | bytes 11899328 | tf_op jit(solution)/shard_map/necf,necd->efd/dot_general | solution.py:60
  104.6 14.6 %copy.40 = bf16[4,384,3584]{2,1,0:T(8,128)(2,1)} copy(bf16[4,384,3584]{1,2,0:T(8,128)(2,1)} %fusion) | data formatting | bytes 22020096
  (7 shorter events, 0.1 us)
Async XLA Ops:
  0.6 97.6 %copy-start = (bf16[4,4,7,384]{3,1,2,0:T(4,128)(2,1)S(1)}, bf16[4,4,7,384]{3,1,2,0:T(4,128)(2,1)}, u32[]{:S(2)}) copy-start(bf16[4,4,7,384]{3,1,2,0:T(4,128)(2,1)} %param.8) | copy-start | bytes 258052
where the time goes:
time: 120 us; the launch traced here: 119 us
  blocking collectives  81.1 us (68%)
  local copies, waits for them, and re-layouts  20.3 us (17%)
  matrix products  14.2 us (12%)
  between operations  2.04 us (2%)
  other arithmetic  1.55 us (1%)
    unnamed x2, blocking collectives  23.7 us
    all_gather x1, blocking collectives, per_device(): lax.all_gather(stacked_rows, 'ctx', axis=0, tiled=True)  19.8 us
    unnamed x12, local copies, waits for them, and re-layouts  18.4 us
    all_gather x1, blocking collectives, per_device(): lax.all_gather(gate_values.astype(jnp.bfloat16), 'ep', axis=0, tiled=True)  10.3 us
    psum x1, blocking collectives, per_device(): whole_terms = lax.psum(partial_value, 'ctx')  9.95 us
    all_gather x1, blocking collectives, per_device(): lax.all_gather(expert_ids, 'ep', axis=0, tiled=True)  8.91 us
    all_gather x1, blocking collectives, per_device(): lax.all_gather(out_grad, 'ep', axis=0, tiled=True)  8.44 us
    dot_general x1, matrix products, per_device(): jnp.einsum('necd,efd->necf', piece_view, w_down, preferred_element_type=j...  7.58 us

commit v1 on v0

--- a/solution.py
+++ b/solution.py
@@ -1,7 +1,23 @@
+import functools
 import jax
 import jax.numpy as jnp
 from jax import lax
 from jax.sharding import PartitionSpec as P
+from jax.lax import axis_size, ppermute
+
+
+def _trace_cycles(z, across):
+    q_n = axis_size(across)
+    f_next, local_next = (z, 0)
+    while 1 << local_next < q_n:
+        high = tuple(((h, h ^ 1 << local_next) for h in range(q_n)))
+        v1 = ppermute(f_next, across, high)
+        f_next = f_next + v1
+        local_next = local_next + 1
+    return f_next
+
+
+_define_patch = functools.partial(_trace_cycles, across="ctx")
 
 
 def route_places(group_ids, experts_all, capacity):
@@ -61,7 +77,7 @@
     hid_grad = hid_piece
     partial_value = gate_piece
     grad_acc, hid_grad, partial_value = (grad_acc, hid_grad, partial_value)
-    whole_terms = lax.psum(partial_value, "ctx")
+    whole_terms = _define_patch(partial_value)
     own_terms = lax.dynamic_slice_in_dim(whole_terms, lax.axis_index("ctx"), 1, 0)
     score_table = lax.all_gather(own_terms.reshape(slots_dev), "ep", axis=0, tiled=True)
     lookup = (

time: 120 us -> 111 us (0.925)
  blocking collectives: 81.1 us -> 71.3 us
  starting transfers between devices: 0 us -> 2.11 us
    psum x1 -> x0, blocking collectives: 9.95 us -> none  [per_device(): whole_terms = lax.psum(partial_value, 'ctx')]
    ppermute x0 -> x2, starting transfers between devices: none -> 2.11 us  [_trace_cycles(): v1 = ppermute(f_next, across, high)]
    all_gather x1, blocking collectives: 8.91 us -> 10.7 us  [per_device(): lax.all_gather(expert_ids, 'ep', axis=0, tiled=True)]
    all_gather x1, blocking collectives: 10.3 us -> 8.61 us  [per_device(): lax.all_gather(gate_values.astype(jnp.bfloat16), 'ep', axis=0, tiled=True)]
    unnamed x12 -> x14, local copies, waits for them, and re-layouts: 18.4 us -> 17.7 us
  transfers between devices with their start and end apart: 0 -> 2, of which waited for: 0 -> 0; matrix products, arithmetic and copies ran while one was open for 0% -> 20% of each run, Pallas kernels for 0% -> 0%
where the time goes in v1:
time: 111 us
  blocking collectives  71.3 us (64%)
  local copies, waits for them, and re-layouts  19.6 us (18%)
  matrix products  14.1 us (13%)
  starting transfers between devices  2.11 us (2%)
  between operations  2.06 us (2%)
  other arithmetic  1.58 us (1%)
    unnamed x2, blocking collectives  23.7 us
    all_gather x1, blocking collectives, per_device(): lax.all_gather(stacked_rows, 'ctx', axis=0, tiled=True)  19.8 us
    unnamed x14, local copies, waits for them, and re-layouts  17.7 us
    all_gather x1, blocking collectives, per_device(): lax.all_gather(expert_ids, 'ep', axis=0, tiled=True)  10.7 us
    all_gather x1, blocking collectives, per_device(): lax.all_gather(gate_values.astype(jnp.bfloat16), 'ep', axis=0, tiled=True)  8.61 us
    all_gather x1, blocking collectives, per_device(): lax.all_gather(out_grad, 'ep', axis=0, tiled=True)  8.44 us
    dot_general x1, matrix products, per_device(): jnp.einsum('necd,efd->necf', piece_view, w_down, preferred_element_type=j...  7.55 us
    dot_general x1, matrix products, per_device(): jnp.einsum('necf,necd->efd', hidden, scaled, preferred_element_type=jnp.f...  6.35 us
  transfers between devices with their start and end apart: 2, of which 0 were waited for; matrix products, arithmetic and copies ran while one was open for 20% of the time, Pallas kernels for 0%

profile of v1, /device:TPU:0, one launch (start us, length us, event | category | flops | bytes accessed | tf_op | source)
XLA Modules:
  0.0 110.8 jit_solution(6288515360543474448)
XLA Ops:
  0.6 0.0 copy-start
  0.6 10.7 %all-gather.2 = s32[8,2,8]{2,1,0:T(2,128)S(1)} all-gather(s32[1,2,8]{2,1,0:T(2,128)} %bitcast.35), channel_id=1, replica_groups=mesh['ctx'=4,'ep'=8] {'ep'}, dimensions={0}, use_global_device_ids=true | all-gather | bytes 576 | tf_op jit(solution)/shard_map/all_gather | solution.py:45
  11.3 0.1 reshape.56
  11.5 0.7 convert_bitcast_fusion
  12.1 8.6 %all-gather.3 = bf16[8,2,8]{2,1,0:T(2,128)(2,1)S(1)} all-gather(bf16[1,2,8]{2,1,0:T(2,128)(2,1)S(1)} %convert_bitcast_fusion), channel_id=1, replica_groups=mesh['ctx'=4,'ep'=8] {'ep'}, dimensions={0}, use_global_device_ids=true | all-gather | bytes 288 | tf_op jit(solution)/shard_map/all_gather | solution.py:46
  20.8 0.1 reshape.61
  20.8 0.1 fusion.9
  20.9 0.2 reduce_window_sum.11
  21.1 0.2 select_reduce_fusion
  21.3 0.1 reduce_sum.49
  21.4 1.2 %dynamic-slice = u32[1]{0:T(128)} dynamic-slice(u32[32]{0:T(128)} %constant.37, u32[]{:T(128)S(6)} %add.28), dynamic_slice_sizes={1} | dynamic-slice | bytes 12
  23.3 0.1 select_reduce_fusion.2
  23.4 0.2 dynamic-update-slice
  23.6 11.9 %all-reduce = bf16[112]{0:T(256)(128)(2,1)S(1)} all-reduce(bf16[112]{0:T(256)(128)(2,1)S(1)} %dynamic-update-slice), channel_id=2, replica_groups=mesh['ctx'=4,'ep'=8] {'ctx'}, use_global_device_ids=true, to_apply=%add | all-reduce | flops 112 | bytes 448
  35.6 0.1 reshape.62
  35.7 0.1 convert_reduce_fusion
  35.8 0.1 copy.33
  35.9 8.4 %all-gather.4 = bf16[8,2,3584]{2,1,0:T(2,128)(2,1)S(1)} all-gather(bf16[1,2,3584]{2,1,0:T(2,128)(2,1)} %bitcast.34), channel_id=1, replica_groups=mesh['ctx'=4,'ep'=8] {'ep'}, dimensions={0}, use_global_device_ids=true | all-gather | bytes 129024 | tf_op jit(solution)/shard_map/all_gather | solution.py:44
  44.4 0.2 fusion.3
  44.7 19.8 %all-gather.5 = bf16[4,28,3584]{2,1,0:T(8,128)(2,1)S(1)} all-gather(bf16[1,28,3584]{2,1,0:T(8,128)(2,1)S(1)} %fusion.3), channel_id=3, replica_groups=mesh['ctx'=4,'ep'=8] {'ctx'}, dimensions={0}, use_global_device_ids=true | all-gather | bytes 1003520 | tf_op jit(solution)/shard_map/all_gather | solution.py:64
  64.5 0.6 copy.34
  65.1 7.6 %multiply_reduce_fusion = (f32[4,4,7]{0,2,1:T(8,128)S(1)}, bf16[4,4,7,384]{3,0,2,1:T(4,128)(2,1)S(1)}) fusion(bf16[4,4,7,384]{3,1,2,0:T(4,128)(2,1)} %param.8, f32[4,4,7]{0,2,1:T(8,128)S(1)} %copy.33, bf16[4,4,7,3584]{3,0,2,1:T(4,128)(2,1)S(1)} %bitcast.31, bf16[4,384,3584]{2,1,0:T(8,128)(2,1)} %param.9), kind=kOutput, calls=%fused_computation.9 | convolution fusion | flops 308496256 | bytes 11985792 | tf_op jit(solution)/shard_map/necd,efd->necf/dot_general | solution.py:72
  72.7 0.1 copy.43
  72.8 0.0 copy-start.1
  72.8 0.0 collective-permute-start
  72.8 0.0 copy-done
  72.8 6.4 %fusion = bf16[4,384,3584]{1,2,0:T(8,128)(2,1)} fusion(bf16[4,4,7,3584]{3,0,2,1:T(4,128)(2,1)S(1)} %bitcast.32, f32[4,4,7]{0,2,1:T(8,128)S(1)} %copy.33, bf16[4,4,7,384]{3,1,2,0:T(4,128)(2,1)S(1)} %copy-done), kind=kOutput, calls=%fused_computation.1 | convolution fusion | flops 314990592 | bytes 11899328 | tf_op jit(solution)/shard_map/necf,necd->efd/dot_general | solution.py:76
  79.2 0.0 collective-permute-done
  79.2 2.1 %collective-permute-start.1 = (f32[4,4,7]{2,0,1:T(4,128)S(1)}, f32[4,4,7]{2,0,1:T(4,128)S(1)}, u32[]{:S(2)}, u32[]{:S(2)}) collective-permute-start(f32[4,4,7]{2,0,1:T(4,128)S(1)} %add.25), channel_id=1, source_target_pairs={{0,16},{8,24},{16,0},{24,8},{1,17},{9,25},{17,1},{25,9},{2,18},{10... | collective-permute-start | bytes 1352 | tf_op jit(solution)/shard_map/ppermute | solution.py:14
  81.3 0.0 copy-done.1
  81.3 0.6 dynamic-slice.1
  82.5 0.7 copy.39
  83.2 14.6 %copy.40 = bf16[4,384,3584]{2,1,0:T(8,128)(2,1)} copy(bf16[4,384,3584]{1,2,0:T(8,128)(2,1)} %fusion) | data formatting | bytes 22020096
  97.8 0.1 dynamic_slice.6
  97.9 0.0 collective-permute-done.1
  97.9 0.1 reshape.71
  98.0 0.2 dynamic-update-slice.1
  98.2 11.8 %all-reduce.1 = f32[224]{0:T(256)S(1)} all-reduce(f32[224]{0:T(256)S(1)} %dynamic-update-slice.1), channel_id=1, replica_groups=mesh['ctx'=4,'ep'=8] {'ep'}, use_global_device_ids=true, to_apply=%add.1 | all-reduce | flops 224 | bytes 1792
  110.0 0.2 select_reduce_fusion.1
  110.2 0.6 reshape.60
  (8 shorter events, 0.1 us)
Async XLA Ops:
  0.6 72.2 %copy-start = (bf16[4,4,7,384]{3,1,2,0:T(4,128)(2,1)S(1)}, bf16[4,4,7,384]{3,1,2,0:T(4,128)(2,1)}, u32[]{:S(2)}) copy-start(bf16[4,4,7,384]{3,1,2,0:T(4,128)(2,1)} %param.8) | copy-start | bytes 258052
  72.8 8.5 %copy-start.1 = (u32[32]{0:T(128)S(1)}, u32[32]{0:T(128)}, u32[]{:S(2)}) copy-start(u32[32]{0:T(128)} %constant.42) | copy-start | bytes 388
  72.8 6.4 %collective-permute-start = (f32[4,4,7]{2,0,1:T(4,128)S(1)}, f32[4,4,7]{2,0,1:T(4,128)S(1)}, u32[]{:S(2)}, u32[]{:S(2)}) collective-permute-start(f32[4,4,7]{2,0,1:T(4,128)S(1)} %copy.43), channel_id=1, source_target_pairs={{0,8},{8,0},{16,24},{24,16},{1,9},{9,1},{17,25},{25,17},{2,10},{10... | collective-permute-start | bytes 1352 | tf_op jit(solution)/shard_map/ppermute | solution.py:14
  79.2 18.7 %collective-permute-start.1 = (f32[4,4,7]{2,0,1:T(4,128)S(1)}, f32[4,4,7]{2,0,1:T(4,128)S(1)}, u32[]{:S(2)}, u32[]{:S(2)}) collective-permute-start(f32[4,4,7]{2,0,1:T(4,128)S(1)} %add.25), channel_id=1, source_target_pairs={{0,16},{8,24},{16,0},{24,8},{1,17},{9,25},{17,1},{25,9},{2,18},{10... | collective-permute-start | bytes 1352 | tf_op jit(solution)/shard_map/ppermute | solution.py:14
